TPU v7x, 32 devices: a whole 2x2x4 slice. The times are simulated.
32 devices in a mesh: prow: 8 (over z, y), pcol: 4 (over x, core).
Axes of the slice: x: 2, y: 2, z: 4, core: 2. Of those that a mesh axis runs over, the one named last changes fastest.
Arguments:
- paper_x: bfloat16 [8192, 768], P(('prow', 'pcol')), may hold values from -6 to 6
- author_x: bfloat16 [4096, 768], P(('pcol', 'prow')), may hold values from -6 to 6
- w_self: bfloat16 [768, 768], replicated, may hold values from -0.21875 to 0.21875
- w_rel: bfloat16 [2, 768, 768], replicated, may hold values from -0.009765625 to 0.009765625
- w_two: bfloat16 [768, 768], replicated, may hold values from -0.0068359375 to 0.0068359375
- block_rows: int32 [8, 4, 32], P('prow', 'pcol'), may hold values from 0 to 7, as said below
- block_cols: int32 [8, 4, 32], P('prow', 'pcol'), may hold values from 0 to 7, as said below
- block_type: int32 [8, 4, 32], P('prow', 'pcol'), may hold values from 0 to 1
- block_count: int32 [8, 4], P('prow', 'pcol'), may hold values from 8 to 32, as said below
- block_vals: bfloat16 [8, 4, 32, 128, 128], P('prow', 'pcol'), may hold values from 0 to 1, as said below
Outputs:
- paper_hidden: bfloat16 [8192, 768], P(('prow', 'pcol'))
- author_out: bfloat16 [4096, 768], P(('pcol', 'prow'))
Inputs may be any that keep to these rules, and one draw needn't show every extreme that they name: `block_rows`: within one tile the live and dead slots name distinct positions; block rows are below 8. `block_cols`: block columns are below 8; with block_rows, positions of one tile are distinct. `block_count`: slots 0 to count - 1 of a tile are live; some tile holds 32 live slots and some tile 32 // 4 in every draw. `block_vals`: every entry is 0 or 1.
All inputs are finite; a program needn't handle non-finite values.
Results may differ from a plain program's by a relative error of at most 0.0041.
Values may be sent and summed in bfloat16 or wider, within the bound.
A program may use at most 64 MiB of HBM per device.

v0:
```python
import jax
import jax.numpy as jnp
from jax import lax
from jax.sharding import PartitionSpec as P

GROUP = 16


def per_device(
    paper_x,
    author_x,
    w_self,
    w_rel,
    w_two,
    block_rows,
    block_cols,
    block_type,
    block_count,
    block_vals,
):
    slots = block_rows.shape[2]
    side = block_vals.shape[3]
    width = paper_x.shape[1]
    relations = w_rel.shape[0]
    groups = slots // GROUP
    own_rows = paper_x.shape[0]
    row_ids = block_rows.reshape(groups, GROUP)
    col_ids = block_cols.reshape(groups, GROUP)
    type_ids = block_type.reshape(groups, GROUP)
    live = (
        (jnp.arange(slots, dtype=jnp.int32) < block_count.reshape(()))
        .astype(jnp.float32)
        .reshape(groups, GROUP)
    )
    contents = block_vals.reshape(groups, GROUP, side, side)
    self_term = jnp.dot(paper_x, w_self, preferred_element_type=jnp.float32)
    authors = lax.all_gather(author_x, "prow", axis=0, tiled=True)
    messages = jnp.stack(
        [
            jnp.dot(authors, w_rel[index], preferred_element_type=jnp.float32)
            for index in range(relations)
        ]
    ).astype(jnp.bfloat16)
    col_blocks = messages.shape[1] // side
    row_blocks = own_rows * lax.axis_size("pcol") // side
    table = messages.reshape(relations * col_blocks, side, width)
    row_range = jnp.arange(row_blocks, dtype=jnp.int32)
    col_range = jnp.arange(col_blocks, dtype=jnp.int32)

    def first_hop(total, item):
        rows_now, cols_now, types_now, mask_now, content_now = item
        picked = table[types_now * col_blocks + cols_now]
        product = jnp.einsum(
            "kpa,kaf->kpf", content_now, picked, preferred_element_type=jnp.float32
        )
        placing = (rows_now[:, None] == row_range[None, :]).astype(jnp.float32) * mask_now[:, None]
        return (
            total + jnp.einsum("kr,kpf->rpf", placing, product, precision=lax.Precision.HIGHEST),
            None,
        )

    start = jnp.zeros((row_blocks, side, width), jnp.float32)
    partial_value, _ = lax.scan(first_hop, start, (row_ids, col_ids, type_ids, live, contents))
    partial_value = partial_value.reshape(row_blocks * side, width)
    summed = lax.psum_scatter(partial_value, "pcol", scatter_dimension=0, tiled=True)
    paper_hidden = jnp.maximum(self_term + summed, 0.0).astype(jnp.bfloat16)
    outgoing = jnp.dot(paper_hidden, w_two, preferred_element_type=jnp.float32).astype(jnp.bfloat16)
    paper_rows = lax.all_gather(outgoing, "pcol", axis=0, tiled=True).reshape(
        row_blocks, side, width
    )

    def second_hop(total, item):
        rows_now, cols_now, mask_now, content_now = item
        picked = paper_rows[rows_now]
        product = jnp.einsum(
            "kpa,kpf->kaf", content_now, picked, preferred_element_type=jnp.float32
        )
        placing = (cols_now[:, None] == col_range[None, :]).astype(jnp.float32) * mask_now[:, None]
        return (
            total + jnp.einsum("kc,kaf->caf", placing, product, precision=lax.Precision.HIGHEST),
            None,
        )

    start_two = jnp.zeros((col_blocks, side, width), jnp.float32)
    author_part, _ = lax.scan(second_hop, start_two, (row_ids, col_ids, live, contents))
    author_total = lax.psum_scatter(
        author_part.reshape(col_blocks * side, width), "prow", scatter_dimension=0, tiled=True
    )
    return (paper_hidden, author_total.astype(jnp.bfloat16))


def solution(mesh):
    return jax.shard_map(
        per_device,
        mesh=mesh,
        in_specs=(
            P(("prow", "pcol"), None),
            P(("pcol", "prow"), None),
            P(),
            P(),
            P(),
            P("prow", "pcol", None),
            P("prow", "pcol", None),
            P("prow", "pcol", None),
            P("prow", "pcol"),
            P("prow", "pcol", None, None, None),
        ),
        out_specs=(P(("prow", "pcol"), None), P(("pcol", "prow"), None)),
        check_vma=False,
    )
```

profile of v0, /device:TPU:0, one launch (start us, length us, event | category | flops | bytes accessed | tf_op | source)
XLA Modules:
  0.0 299.5 jit_solution(3397042512454895330)
XLA Ops:
  7.2 0.7 all-gather.3.cloned.1.call-update
  8.0 0.5 broadcast.116
  8.5 1.3 reduce.9
  9.9 1.3 reduce.11
  11.3 1.3 reduce.10
  13.4 43.8 %all-gather.3.cloned.1.call-done = bf16[1024,768]{1,0:T(8,128)(2,1)} async-done(((bf16[128,768]{1,0:T(8,128)(2,1)}), bf16[1024,768]{1,0:T(8,128)(2,1)}) %all-gather.3.cloned.1.call-update) | async-done | bytes 1572880 | tf_op jit(solution)/shard_map/all_gather | solution.py:37
  57.1 3.3 %fusion.41 = bf16[1,1024,768]{2,1,0:T(8,128)(2,1)S(1)} fusion(bf16[1024,768]{1,0:T(8,128)(2,1)} %all-gather.3.cloned.1.call-done, bf16[2,768,768]{2,1,0:T(8,128)(2,1)} %param.17), kind=kOutput, calls=%fused_computation.55 | convolution fusion | flops 1208745984 | bytes 4325376 | tf_op jit(solution)/shard_map/dot_general | solution.py:40
  60.4 1.4 fusion.42
  61.8 2.0 pad_maximum_fusion
  63.8 41.9 %while.22 = (s32[]{:T(128)}, f32[8,128,768]{2,0,1:T(8,128)}, s32[2,16]{1,0:T(2,128)S(1)}, f32[2,16]{1,0:T(2,128)S(1)}, bf16[2,16,128,128]{3,2,1,0:T(8,128)(2,1)S...) while((s32[]{:T(128)}, f32[8,128,768]{2,0,1:T(8,128)}, ...), condition=%wide.region_1.2_spmd.clone, body=%wide.region_0.1_spmd.clone.sunk | while | flops 555222400 | bytes 28840768 | solution.py:63
  63.8 4.3 %gather_fusion = bf16[16,128,768]{2,1,0:T(8,128)(2,1)} fusion(bf16[16,128,768]{2,1,0:T(8,128)(2,1)} %get-tuple-element.297, s32[1024]{0:T(1024)S(1)} %pad_clamp_fusion.4), kind=kCustom, calls=%fused_computation.clone.clone.1 | custom fusion | bytes 6291520 | tf_op jit(solution)/shard_map/while/body/eval_jaxpr/gather | solution.py:52
  68.1 5.5 %fusion.78 = f32[16,128,768]{2,1,0:T(8,128)} fusion(bf16[16,128,768]{2,1,0:T(8,128)(2,1)} %gather_fusion, bf16[2,16,128,128]{3,2,1,0:T(8,128)(2,1)S(1)} %get-tuple-element.294, s32[]{:T(128)} %get-tuple-element.280), kind=kOutput, calls=%fused_computation.7.clone.1 | convolution fusion | flops 402653184 | bytes 9961476 | tf_op jit(solution)/shard_map/while/body/eval_jaxpr/kpa,kaf->kpf/dot_general | solution.py:53
  73.6 10.9 %select_add_fusion.4 = f32[8,128,768]{2,0,1:T(8,128)} fusion(f32[8,128,768]{2,0,1:T(8,128)} %get-tuple-element.281, f32[16,128,768]{2,1,0:T(8,128)} %fusion.78, pred[]{:T(512)S(6)} %compare.6, f32[16]{0:T(128)S(1)} %fusion.79, s32[16]{0:T(128)S(1)} %fusion.80), kind=kOutput, calls=%fused_computation.6.clone.1 | convolution fusion | flops 152568064 | bytes 12583041 | tf_op jit(solution)/shard_map/while/body/eval_jaxpr/kr,kpf->rpf/dot_general | solution.py:58
  84.5 4.3 %gather_fusion = bf16[16,128,768]{2,1,0:T(8,128)(2,1)} fusion(bf16[16,128,768]{2,1,0:T(8,128)(2,1)} %get-tuple-element.297, s32[1024]{0:T(1024)S(1)} %pad_clamp_fusion.4), kind=kCustom, calls=%fused_computation.clone.clone.1 | custom fusion | bytes 6291520 | tf_op jit(solution)/shard_map/while/body/eval_jaxpr/gather | solution.py:52
  88.8 5.5 %fusion.78 = f32[16,128,768]{2,1,0:T(8,128)} fusion(bf16[16,128,768]{2,1,0:T(8,128)(2,1)} %gather_fusion, bf16[2,16,128,128]{3,2,1,0:T(8,128)(2,1)S(1)} %get-tuple-element.294, s32[]{:T(128)} %get-tuple-element.280), kind=kOutput, calls=%fused_computation.7.clone.1 | convolution fusion | flops 402653184 | bytes 9961476 | tf_op jit(solution)/shard_map/while/body/eval_jaxpr/kpa,kaf->kpf/dot_general | solution.py:53
  94.3 11.4 %select_add_fusion.4 = f32[8,128,768]{2,0,1:T(8,128)} fusion(f32[8,128,768]{2,0,1:T(8,128)} %get-tuple-element.281, f32[16,128,768]{2,1,0:T(8,128)} %fusion.78, pred[]{:T(512)S(6)} %compare.6, f32[16]{0:T(128)S(1)} %fusion.79, s32[16]{0:T(128)S(1)} %fusion.80), kind=kOutput, calls=%fused_computation.6.clone.1 | convolution fusion | flops 152568064 | bytes 12583041 | tf_op jit(solution)/shard_map/while/body/eval_jaxpr/kr,kpf->rpf/dot_general | solution.py:58
  105.7 4.6 %copy.12 = f32[8,128,768]{2,1,0:T(8,128)} copy(f32[8,128,768]{2,0,1:T(8,128)} %get-tuple-element.91) | data formatting | bytes 6291456 | tf_op jit(solution)/shard_map/while | solution.py:63
  110.3 36.3 %reduce-scatter.3.cloned.1.call-done = f32[256,768]{1,0:T(8,128)} async-done(((f32[1024,768]{1,0:T(8,128)}), f32[256,768]{1,0:T(8,128)}) %reduce-scatter.3.cloned.1.call-update) | async-done | bytes 786448 | tf_op jit(solution)/shard_map/reduce_scatter | solution.py:65
  146.7 1.6 fusion.44
  148.3 2.6 convolution_convert_fusion.2
  151.0 0.2 reduce-scatter.5.cloned.1.call-start
  151.2 19.5 %all-gather.5.cloned.1.call-done = bf16[1024,768]{1,0:T(8,128)(2,1)} async-done(((bf16[256,768]{1,0:T(8,128)(2,1)}), bf16[1024,768]{1,0:T(8,128)(2,1)}) %all-gather.5.cloned.1.call-update) | async-done | bytes 1572880 | tf_op jit(solution)/shard_map/all_gather | solution.py:68
  170.8 41.2 %while.23 = (s32[]{:T(128)}, f32[8,128,768]{2,0,1:T(8,128)}, s32[2,16]{1,0:T(2,128)S(1)}, f32[2,16]{1,0:T(2,128)S(1)}, bf16[2,16,128,128]{3,2,1,0:T(8,128)(2,1)S...) while((s32[]{:T(128)}, f32[8,128,768]{2,0,1:T(8,128)}, ...), condition=%wide.region_4.5_spmd.clone, body=%wide.region_3.4_spmd.clone.sunk | while | flops 555222336 | bytes 28840696 | solution.py:85
  170.8 3.8 %gather_fusion.1 = bf16[16,128,768]{2,1,0:T(8,128)(2,1)} fusion(bf16[8,128,768]{2,1,0:T(8,128)(2,1)} %get-tuple-element.324, s32[1024]{0:T(1024)S(1)} %pad_clamp_fusion.5), kind=kCustom, calls=%fused_computation.1.clone.clone.1 | custom fusion | bytes 6291520 | tf_op jit(solution)/shard_map/while/body/eval_jaxpr/gather | solution.py:74
  174.6 5.6 %fusion.86 = f32[16,128,768]{2,1,0:T(8,128)} fusion(bf16[16,128,768]{2,1,0:T(8,128)(2,1)} %gather_fusion.1, bf16[2,16,128,128]{3,2,1,0:T(8,128)(2,1)S(1)} %get-tuple-element.322, s32[]{:T(128)} %get-tuple-element.309), kind=kOutput, calls=%fused_computation.32.clone.1 | convolution fusion | flops 402653184 | bytes 9961476 | tf_op jit(solution)/shard_map/while/body/eval_jaxpr/kpa,kpf->kaf/dot_general | solution.py:75
  180.2 11.0 %select_add_fusion.5 = f32[8,128,768]{2,0,1:T(8,128)} fusion(f32[8,128,768]{2,0,1:T(8,128)} %get-tuple-element.310, f32[16,128,768]{2,1,0:T(8,128)} %fusion.86, pred[]{:T(512)S(6)} %compare.7, f32[16]{0:T(128)S(1)} %fusion.87, s32[16]{0:T(128)S(1)} %fusion.88), kind=kOutput, calls=%fused_computation.31.clone.1 | convolution fusion | flops 152568064 | bytes 12583041 | tf_op jit(solution)/shard_map/while/body/eval_jaxpr/kc,kaf->caf/dot_general | solution.py:80
  191.2 3.8 %gather_fusion.1 = bf16[16,128,768]{2,1,0:T(8,128)(2,1)} fusion(bf16[8,128,768]{2,1,0:T(8,128)(2,1)} %get-tuple-element.324, s32[1024]{0:T(1024)S(1)} %pad_clamp_fusion.5), kind=kCustom, calls=%fused_computation.1.clone.clone.1 | custom fusion | bytes 6291520 | tf_op jit(solution)/shard_map/while/body/eval_jaxpr/gather | solution.py:74
  195.0 5.6 %fusion.86 = f32[16,128,768]{2,1,0:T(8,128)} fusion(bf16[16,128,768]{2,1,0:T(8,128)(2,1)} %gather_fusion.1, bf16[2,16,128,128]{3,2,1,0:T(8,128)(2,1)S(1)} %get-tuple-element.322, s32[]{:T(128)} %get-tuple-element.309), kind=kOutput, calls=%fused_computation.32.clone.1 | convolution fusion | flops 402653184 | bytes 9961476 | tf_op jit(solution)/shard_map/while/body/eval_jaxpr/kpa,kpf->kaf/dot_general | solution.py:75
  200.5 11.4 %select_add_fusion.5 = f32[8,128,768]{2,0,1:T(8,128)} fusion(f32[8,128,768]{2,0,1:T(8,128)} %get-tuple-element.310, f32[16,128,768]{2,1,0:T(8,128)} %fusion.86, pred[]{:T(512)S(6)} %compare.7, f32[16]{0:T(128)S(1)} %fusion.87, s32[16]{0:T(128)S(1)} %fusion.88), kind=kOutput, calls=%fused_computation.31.clone.1 | convolution fusion | flops 152568064 | bytes 12583041 | tf_op jit(solution)/shard_map/while/body/eval_jaxpr/kc,kaf->caf/dot_general | solution.py:80
  212.0 4.6 %copy.13 = f32[8,128,768]{2,1,0:T(8,128)} copy(f32[8,128,768]{2,0,1:T(8,128)} %get-tuple-element.92) | data formatting | bytes 6291456 | tf_op jit(solution)/shard_map/while | solution.py:85
  216.5 74.7 %reduce-scatter.5.cloned.1.call-done = f32[128,768]{1,0:T(8,128)} async-done(((f32[1024,768]{1,0:T(8,128)}), f32[128,768]{1,0:T(8,128)}) %reduce-scatter.5.cloned.1.call-update) | async-done | bytes 393232 | tf_op jit(solution)/shard_map/reduce_scatter | solution.py:86
  291.2 1.7 convert_element_type.24
  (40 shorter events, 0.6 us)
Async XLA Ops:
  7.2 139.5 %copy-start = (bf16[768,768]{1,0:T(8,128)(2,1)S(1)}, bf16[768,768]{1,0:T(8,128)(2,1)}, u32[]{:S(2)}) copy-start(bf16[768,768]{1,0:T(8,128)(2,1)} %param.16) | copy-start | bytes 3538948
  7.2 49.9 %all-gather.3.cloned.1.call-start = ((), (), s32[]{:S(2)}) async-start(), calls=%async_computation.2 | async-start | bytes 1769472 | tf_op jit(solution)/shard_map/all_gather | solution.py:37
  7.9 138.8 %reduce-scatter.3.cloned.1.call-start = ((), (), s32[]{:S(2)}) async-start(), calls=%async_computation.3 | async-start | bytes 3932160 | tf_op jit(solution)/shard_map/reduce_scatter | solution.py:65
  57.1 3.3 %copy-start.4 = (bf16[2,768,768]{2,1,0:T(8,128)(2,1)S(1)}, bf16[2,768,768]{2,1,0:T(8,128)(2,1)}, u32[]{:S(2)}) copy-start(bf16[2,768,768]{2,1,0:T(8,128)(2,1)} %param.17) | copy-start | bytes 7077892
  57.1 3.3 %copy-start.5 = (bf16[1024,768]{1,0:T(8,128)(2,1)S(1)}, bf16[1024,768]{1,0:T(8,128)(2,1)}, u32[]{:S(2)}) copy-start(bf16[1024,768]{1,0:T(8,128)(2,1)} %all-gather.3.cloned.1.call-done) | copy-start | bytes 4718596
  61.8 2.0 copy-start.1
  110.3 36.4 %copy-start.3 = (bf16[256,768]{1,0:T(8,128)(2,1)S(1)}, bf16[256,768]{1,0:T(8,128)(2,1)}, u32[]{:S(2)}) copy-start(bf16[256,768]{1,0:T(8,128)(2,1)} %param.14) | copy-start | bytes 1179652
  110.3 60.5 %all-gather.5.cloned.1.call-start = ((), (), s32[]{:S(2)}) async-start(), calls=%async_computation.4 | async-start | bytes 1966080 | tf_op jit(solution)/shard_map/all_gather | solution.py:68
  148.3 22.5 %copy-start.2 = (bf16[256,768]{1,0:T(8,128)(2,1)}, bf16[256,768]{1,0:T(8,128)(2,1)S(1)}, u32[]{:S(2)}) copy-start(bf16[256,768]{1,0:T(8,128)(2,1)S(1)} %fusion.44) | copy-start | bytes 1179652
  151.0 140.3 %reduce-scatter.5.cloned.1.call-start = ((), (), s32[]{:S(2)}) async-start(), calls=%async_computation.5 | async-start | bytes 3538944 | tf_op jit(solution)/shard_map/reduce_scatter | solution.py:86
Sparse Core Ops, SparseCore 0:
  10.2 46.8 all-gather.2
  110.4 36.2 reduce-scatter.2
  151.1 19.6 all-gather.4
  216.7 74.5 reduce-scatter.4
where the time goes:
time: 300 us; the launch traced here: 299 us
  waiting for transfers between devices  175 us (58%)
  matrix products  75.7 us (25%)
  local copies, waits for them, and re-layouts  26.1 us (9%)
  between operations  14.5 us (5%)
  other arithmetic  7.68 us (3%)
    reduce_scatter x1, waiting for transfers between devices, per_device(): lax.psum_scatter(author_part.reshape(col_blocks * side, width), 'prow', s...  74.7 us
    all_gather x1, waiting for transfers between devices, per_device(): authors = lax.all_gather(author_x, 'prow', axis=0, tiled=True)  43.8 us
    reduce_scatter x1, waiting for transfers between devices, per_device(): lax.psum_scatter(partial_value, 'pcol', scatter_dimension=0, tiled=True)  36.3 us
    dot_general x2, matrix products, second_hop(): jnp.einsum('kc,kaf->caf', placing, product, precision=lax.Precision.HIGHEST)  22.4 us
    dot_general x2, matrix products, first_hop(): jnp.einsum('kr,kpf->rpf', placing, product, precision=lax.Precision.HIGHEST)  22.3 us
    all_gather x1, waiting for transfers between devices, per_device(): lax.all_gather(outgoing, 'pcol', axis=0, tiled=True)  19.5 us
    dot_general x2, matrix products, second_hop(): jnp.einsum('kpa,kpf->kaf', content_now, picked, preferred_element_type=jn...  11.1 us
    dot_general x2, matrix products, first_hop(): jnp.einsum('kpa,kaf->kpf', content_now, picked, preferred_element_type=jn...  11 us
  transfers between devices with their start and end apart: 4, of which 4 were waited for; matrix products, arithmetic and copies ran while one was open for 2% of the time, Pallas kernels for 0%

commit v1 on v0

--- a/solution.py
+++ b/solution.py
@@ -1,9 +1,39 @@
+import functools
 import jax
 import jax.numpy as jnp
 from jax import lax
 from jax.sharding import PartitionSpec as P
 
 GROUP = 16
+
+
+def table_handle(base_x, axis_tag):
+    z_new = lax.axis_size(axis_tag)
+    moved, found_now, tile_out = (z_new, lax.axis_index(axis_tag), base_x.shape[0])
+    sheets = []
+    for i0 in [*range(moved)]:
+        sheets.append((i0, (i0 + 1) % moved))
+    leaves = []
+    for i0 in tuple(range(moved)):
+        leaves.append((i0, (i0 - 1) % moved))
+    u1 = jnp.zeros((*base_x.shape[:0], moved * tile_out, *base_x.shape[1:]), base_x.dtype)
+    u1 = lax.dynamic_update_slice_in_dim(u1, base_x, found_now * tile_out, axis=0)
+    frame_out = f_next = base_x
+    last = moved // 2
+    for num in tuple(range(1, last + 1)):
+        frame_out = lax.ppermute(frame_out, axis_tag, sheets)
+        u1 = lax.dynamic_update_slice_in_dim(
+            u1, frame_out, (found_now - num) % moved * tile_out, axis=0
+        )
+        if num < moved - last:
+            f_next = lax.ppermute(f_next, axis_tag, leaves)
+            u1 = lax.dynamic_update_slice_in_dim(
+                u1, f_next, (found_now + num) % moved * tile_out, axis=0
+            )
+    return u1
+
+
+meet_samples = functools.partial(table_handle, axis_tag="pcol")
 
 
 def per_device(
@@ -65,9 +95,7 @@
     summed = lax.psum_scatter(partial_value, "pcol", scatter_dimension=0, tiled=True)
     paper_hidden = jnp.maximum(self_term + summed, 0.0).astype(jnp.bfloat16)
     outgoing = jnp.dot(paper_hidden, w_two, preferred_element_type=jnp.float32).astype(jnp.bfloat16)
-    paper_rows = lax.all_gather(outgoing, "pcol", axis=0, tiled=True).reshape(
-        row_blocks, side, width
-    )
+    paper_rows = meet_samples(outgoing).reshape(row_blocks, side, width)
 
     def second_hop(total, item):
         rows_now, cols_now, mask_now, content_now = item

time: 300 us -> 295 us (0.983)
  waiting for transfers between devices: 175 us -> 170 us
    all_gather x1 -> x0, waiting for transfers between devices: 19.5 us -> none  [per_device(): lax.all_gather(outgoing, 'pcol', axis=0, tiled=True)]
    ppermute x0 -> x3, waiting for transfers between devices: none -> 14.6 us  [the longest x2 14.6 us: table_handle(): frame_out = lax.ppermute(frame_out, axis_tag, sheets)]
    dynamic_update_slice x0 -> x3, local copies, waits for them, and re-layouts: none -> 3.08 us  [the longest x2 2.05 us: table_handle(): lax.dynamic_update_slice_in_dim(u1, frame_out, (found_now - num) % moved...]
  transfers between devices with their start and end apart: 4 -> 6, of which waited for: 4 -> 5; matrix products, arithmetic and copies ran while one was open for 2% -> 2% of each run, Pallas kernels for 0% -> 0%
where the time goes in v1:
time: 295 us
  waiting for transfers between devices  170 us (58%)
  matrix products  74.1 us (25%)
  local copies, waits for them, and re-layouts  26.5 us (9%)
  between operations  14.5 us (5%)
  other arithmetic  7.69 us (3%)
    reduce_scatter x1, waiting for transfers between devices, per_device(): lax.psum_scatter(author_part.reshape(col_blocks * side, width), 'prow', s...  74.4 us
    all_gather x1, waiting for transfers between devices, per_device(): authors = lax.all_gather(author_x, 'prow', axis=0, tiled=True)  43.8 us
    reduce_scatter x1, waiting for transfers between devices, per_device(): lax.psum_scatter(partial_value, 'pcol', scatter_dimension=0, tiled=True)  36.3 us
    dot_general x2, matrix products, first_hop(): jnp.einsum('kr,kpf->rpf', placing, product, precision=lax.Precision.HIGHEST)  22.4 us
    dot_general x2, matrix products, second_hop(): jnp.einsum('kc,kaf->caf', placing, product, precision=lax.Precision.HIGHEST)  22.4 us
    ppermute x2, waiting for transfers between devices, table_handle(): frame_out = lax.ppermute(frame_out, axis_tag, sheets)  14.6 us
    dot_general x2, matrix products, second_hop(): jnp.einsum('kpa,kpf->kaf', content_now, picked, preferred_element_type=jn...  11.5 us
    dot_general x2, matrix products, first_hop(): jnp.einsum('kpa,kaf->kpf', content_now, picked, preferred_element_type=jn...  11 us
  transfers between devices with their start and end apart: 6, of which 5 were waited for; matrix products, arithmetic and copies ran while one was open for 2% of the time, Pallas kernels for 0%

profile of v1, /device:TPU:0, one launch (start us, length us, event | category | flops | bytes accessed | tf_op | source)
XLA Modules:
  0.0 294.5 jit_solution(13100173751352111013)
XLA Ops:
  8.5 1.3 reduce.9
  10.5 1.3 reduce.10
  11.9 1.3 reduce.11
  13.4 43.8 %all-gather.2.cloned.1.call-done = bf16[1024,768]{1,0:T(8,128)(2,1)} async-done(((bf16[128,768]{1,0:T(8,128)(2,1)}), bf16[1024,768]{1,0:T(8,128)(2,1)}) %all-gather.2.cloned.1.call-update) | async-done | bytes 1572880 | tf_op jit(solution)/shard_map/all_gather | solution.py:67
  57.1 3.3 %fusion.42 = bf16[1,1024,768]{2,1,0:T(8,128)(2,1)S(1)} fusion(bf16[1024,768]{1,0:T(8,128)(2,1)} %all-gather.2.cloned.1.call-done, bf16[2,768,768]{2,1,0:T(8,128)(2,1)} %param.17), kind=kOutput, calls=%fused_computation.56 | convolution fusion | flops 1208745984 | bytes 4325376 | tf_op jit(solution)/shard_map/dot_general | solution.py:70
  60.4 1.4 fusion.41
  61.8 2.0 pad_maximum_fusion
  63.8 42.1 %while.22 = (s32[]{:T(128)}, f32[8,128,768]{2,0,1:T(8,128)}, s32[2,16]{1,0:T(2,128)S(1)}, f32[2,16]{1,0:T(2,128)S(1)}, bf16[2,16,128,128]{3,2,1,0:T(8,128)(2,1)S...) while((s32[]{:T(128)}, f32[8,128,768]{2,0,1:T(8,128)}, ...), condition=%wide.region_1.2_spmd.clone, body=%wide.region_0.1_spmd.clone.sunk | while | flops 555222400 | bytes 28840776 | solution.py:93
  63.8 4.3 %gather_fusion = bf16[16,128,768]{2,1,0:T(8,128)(2,1)} fusion(bf16[16,128,768]{2,1,0:T(8,128)(2,1)} %get-tuple-element.299, s32[1024]{0:T(1024)S(1)} %pad_clamp_fusion.4), kind=kCustom, calls=%fused_computation.clone.clone.1 | custom fusion | bytes 6291520 | tf_op jit(solution)/shard_map/while/body/eval_jaxpr/gather | solution.py:82
  68.1 5.5 %fusion.78 = f32[16,128,768]{2,1,0:T(8,128)} fusion(bf16[16,128,768]{2,1,0:T(8,128)(2,1)} %gather_fusion, bf16[2,16,128,128]{3,2,1,0:T(8,128)(2,1)S(1)} %get-tuple-element.296, s32[]{:T(128)S(6)} %copy.30), kind=kOutput, calls=%fused_computation.7.clone.1 | convolution fusion | flops 402653184 | bytes 9961476 | tf_op jit(solution)/shard_map/while/body/eval_jaxpr/kpa,kaf->kpf/dot_general | solution.py:83
  73.6 11.0 %select_add_fusion.4 = f32[8,128,768]{2,0,1:T(8,128)} fusion(f32[8,128,768]{2,0,1:T(8,128)} %get-tuple-element.283, f32[16,128,768]{2,1,0:T(8,128)} %fusion.78, pred[]{:T(512)S(6)} %compare.9, f32[16]{0:T(128)S(1)} %fusion.79, s32[16]{0:T(128)S(1)} %fusion.80), kind=kOutput, calls=%fused_computation.6.clone.1 | convolution fusion | flops 152568064 | bytes 12583041 | tf_op jit(solution)/shard_map/while/body/eval_jaxpr/kr,kpf->rpf/dot_general | solution.py:88
  84.7 4.3 %gather_fusion = bf16[16,128,768]{2,1,0:T(8,128)(2,1)} fusion(bf16[16,128,768]{2,1,0:T(8,128)(2,1)} %get-tuple-element.299, s32[1024]{0:T(1024)S(1)} %pad_clamp_fusion.4), kind=kCustom, calls=%fused_computation.clone.clone.1 | custom fusion | bytes 6291520 | tf_op jit(solution)/shard_map/while/body/eval_jaxpr/gather | solution.py:82
  88.9 5.5 %fusion.78 = f32[16,128,768]{2,1,0:T(8,128)} fusion(bf16[16,128,768]{2,1,0:T(8,128)(2,1)} %gather_fusion, bf16[2,16,128,128]{3,2,1,0:T(8,128)(2,1)S(1)} %get-tuple-element.296, s32[]{:T(128)S(6)} %copy.30), kind=kOutput, calls=%fused_computation.7.clone.1 | convolution fusion | flops 402653184 | bytes 9961476 | tf_op jit(solution)/shard_map/while/body/eval_jaxpr/kpa,kaf->kpf/dot_general | solution.py:83
  94.5 11.5 %select_add_fusion.4 = f32[8,128,768]{2,0,1:T(8,128)} fusion(f32[8,128,768]{2,0,1:T(8,128)} %get-tuple-element.283, f32[16,128,768]{2,1,0:T(8,128)} %fusion.78, pred[]{:T(512)S(6)} %compare.9, f32[16]{0:T(128)S(1)} %fusion.79, s32[16]{0:T(128)S(1)} %fusion.80), kind=kOutput, calls=%fused_computation.6.clone.1 | convolution fusion | flops 152568064 | bytes 12583041 | tf_op jit(solution)/shard_map/while/body/eval_jaxpr/kr,kpf->rpf/dot_general | solution.py:88
  105.9 4.5 %copy.12 = f32[8,128,768]{2,1,0:T(8,128)} copy(f32[8,128,768]{2,0,1:T(8,128)} %get-tuple-element.91) | data formatting | bytes 6291456 | tf_op jit(solution)/shard_map/while | solution.py:93
  110.5 36.3 %reduce-scatter.3.cloned.1.call-done = f32[256,768]{1,0:T(8,128)} async-done(((f32[1024,768]{1,0:T(8,128)}), f32[256,768]{1,0:T(8,128)}) %reduce-scatter.3.cloned.1.call-update) | async-done | bytes 786448 | tf_op jit(solution)/shard_map/reduce_scatter | solution.py:95
  146.9 1.6 fusion.44
  149.2 1.7 collective-permute-start.1
  150.9 9.1 %collective-permute-done = bf16[256,768]{1,0:T(8,128)(2,1)} collective-permute-done((bf16[256,768]{1,0:T(8,128)(2,1)S(1)}, bf16[256,768]{1,0:T(8,128)(2,1)}, u32[]{:S(2)}, u32[]{:S(2)}) %collective-permute-start) | collective-permute-done | bytes 393248 | tf_op jit(solution)/shard_map/ppermute | solution.py:24
  160.1 1.0 constant_dynamic-update-slice_fusion.2
  161.1 1.0 constant_dynamic-update-slice_fusion.1
  162.1 5.4 %collective-permute-done.2 = bf16[256,768]{1,0:T(8,128)(2,1)} collective-permute-done((bf16[256,768]{1,0:T(8,128)(2,1)}, bf16[256,768]{1,0:T(8,128)(2,1)}, u32[]{:S(2)}, u32[]{:S(2)}) %collective-permute-start.2) | collective-permute-done | bytes 393248 | tf_op jit(solution)/shard_map/ppermute | solution.py:24
  168.6 38.8 %while.23 = (s32[]{:T(128)}, f32[8,128,768]{2,0,1:T(8,128)}, s32[2,16]{1,0:T(2,128)S(1)}, f32[2,16]{1,0:T(2,128)S(1)}, bf16[2,16,128,128]{3,2,1,0:T(8,128)(2,1)}...) while((s32[]{:T(128)}, f32[8,128,768]{2,0,1:T(8,128)}, ...), condition=%wide.region_4.5_spmd.clone, body=%wide.region_3.4_spmd.clone.sunk | while | flops 555222336 | bytes 28840704 | solution.py:113
  168.6 2.4 gather_fusion.1
  171.0 5.7 %fusion.86 = f32[16,128,768]{2,1,0:T(8,128)} fusion(bf16[16,128,768]{2,1,0:T(8,128)(2,1)} %gather_fusion.1, bf16[2,16,128,128]{3,2,1,0:T(8,128)(2,1)} %get-tuple-element.324, s32[]{:T(128)S(6)} %copy.40), kind=kOutput, calls=%fused_computation.32.clone.1 | convolution fusion | flops 402653184 | bytes 9961476 | tf_op jit(solution)/shard_map/while/body/eval_jaxpr/kpa,kpf->kaf/dot_general | solution.py:103
  176.8 11.0 %select_add_fusion.5 = f32[8,128,768]{2,0,1:T(8,128)} fusion(f32[8,128,768]{2,0,1:T(8,128)} %get-tuple-element.312, f32[16,128,768]{2,1,0:T(8,128)} %fusion.86, pred[]{:T(512)S(6)} %compare.10, f32[16]{0:T(128)S(1)} %fusion.87, s32[16]{0:T(128)S(1)} %fusion.88), kind=kOutput, calls=%fused_computation.31.clone.1 | convolution fusion | flops 152568064 | bytes 12583041 | tf_op jit(solution)/shard_map/while/body/eval_jaxpr/kc,kaf->caf/dot_general | solution.py:108
  187.8 2.4 gather_fusion.1
  190.2 5.7 %fusion.86 = f32[16,128,768]{2,1,0:T(8,128)} fusion(bf16[16,128,768]{2,1,0:T(8,128)(2,1)} %gather_fusion.1, bf16[2,16,128,128]{3,2,1,0:T(8,128)(2,1)} %get-tuple-element.324, s32[]{:T(128)S(6)} %copy.40), kind=kOutput, calls=%fused_computation.32.clone.1 | convolution fusion | flops 402653184 | bytes 9961476 | tf_op jit(solution)/shard_map/while/body/eval_jaxpr/kpa,kpf->kaf/dot_general | solution.py:103
  195.9 11.4 %select_add_fusion.5 = f32[8,128,768]{2,0,1:T(8,128)} fusion(f32[8,128,768]{2,0,1:T(8,128)} %get-tuple-element.312, f32[16,128,768]{2,1,0:T(8,128)} %fusion.86, pred[]{:T(512)S(6)} %compare.10, f32[16]{0:T(128)S(1)} %fusion.87, s32[16]{0:T(128)S(1)} %fusion.88), kind=kOutput, calls=%fused_computation.31.clone.1 | convolution fusion | flops 152568064 | bytes 12583041 | tf_op jit(solution)/shard_map/while/body/eval_jaxpr/kc,kaf->caf/dot_general | solution.py:108
  207.4 4.5 %copy.13 = f32[8,128,768]{2,1,0:T(8,128)} copy(f32[8,128,768]{2,0,1:T(8,128)} %get-tuple-element.92) | data formatting | bytes 6291456 | tf_op jit(solution)/shard_map/while | solution.py:113
  211.9 74.4 %reduce-scatter.5.cloned.1.call-done = f32[128,768]{1,0:T(8,128)} async-done(((f32[1024,768]{1,0:T(8,128)}), f32[128,768]{1,0:T(8,128)}) %reduce-scatter.5.cloned.1.call-update) | async-done | bytes 393232 | tf_op jit(solution)/shard_map/reduce_scatter | solution.py:114
  286.3 1.7 convert_element_type.24
  (49 shorter events, 3.4 us)
Async XLA Ops:
  7.2 141.5 %copy-start = (bf16[768,768]{1,0:T(8,128)(2,1)S(1)}, bf16[768,768]{1,0:T(8,128)(2,1)}, u32[]{:S(2)}) copy-start(bf16[768,768]{1,0:T(8,128)(2,1)} %param.18) | copy-start | bytes 3538948
  7.2 49.9 %all-gather.2.cloned.1.call-start = ((), (), s32[]{:S(2)}) async-start(), calls=%async_computation.2 | async-start | bytes 1769472 | tf_op jit(solution)/shard_map/all_gather | solution.py:67
  7.9 139.0 %reduce-scatter.3.cloned.1.call-start = ((), (), s32[]{:S(2)}) async-start(), calls=%async_computation.3 | async-start | bytes 3932160 | tf_op jit(solution)/shard_map/reduce_scatter | solution.py:95
  57.1 3.3 %copy-start.5 = (bf16[2,768,768]{2,1,0:T(8,128)(2,1)S(1)}, bf16[2,768,768]{2,1,0:T(8,128)(2,1)}, u32[]{:S(2)}) copy-start(bf16[2,768,768]{2,1,0:T(8,128)(2,1)} %param.17) | copy-start | bytes 7077892
  57.1 3.3 %copy-start.6 = (bf16[1024,768]{1,0:T(8,128)(2,1)S(1)}, bf16[1024,768]{1,0:T(8,128)(2,1)}, u32[]{:S(2)}) copy-start(bf16[1024,768]{1,0:T(8,128)(2,1)} %all-gather.2.cloned.1.call-done) | copy-start | bytes 4718596
  61.8 2.0 copy-start.1
  110.5 36.4 %copy-start.3 = (bf16[768,768]{1,0:T(8,128)(2,1)S(1)}, bf16[768,768]{1,0:T(8,128)(2,1)}, u32[]{:S(2)}) copy-start(bf16[768,768]{1,0:T(8,128)(2,1)} %param.16) | copy-start | bytes 3538948
  110.5 36.4 %copy-start.4 = (bf16[256,768]{1,0:T(8,128)(2,1)S(1)}, bf16[256,768]{1,0:T(8,128)(2,1)}, u32[]{:S(2)}) copy-start(bf16[256,768]{1,0:T(8,128)(2,1)} %param.14) | copy-start | bytes 1179652
  110.5 175.8 %reduce-scatter.5.cloned.1.call-start = ((), (), s32[]{:S(2)}) async-start(), calls=%async_computation.4 | async-start | bytes 3538944 | tf_op jit(solution)/shard_map/reduce_scatter | solution.py:114
  148.5 20.1 %copy-start.2 = (bf16[256,768]{1,0:T(8,128)(2,1)}, bf16[256,768]{1,0:T(8,128)(2,1)S(1)}, u32[]{:S(2)}) copy-start(bf16[256,768]{1,0:T(8,128)(2,1)S(1)} %fusion.44) | copy-start | bytes 1179652
  149.1 10.9 %collective-permute-start = (bf16[256,768]{1,0:T(8,128)(2,1)S(1)}, bf16[256,768]{1,0:T(8,128)(2,1)}, u32[]{:S(2)}, u32[]{:S(2)}) collective-permute-start(bf16[256,768]{1,0:T(8,128)(2,1)S(1)} %get-tuple-element.179), channel_id=1, source_target_pairs={{0,1},{1,2},{2,3},{3,0},{4,5},{5,6},{6,7},{7,4},{8,9},{9,10},{10,1... | collective-permute-start | bytes 1179656 | tf_op jit(solution)/shard_map/ppermute | solution.py:24
  149.2 11.9 %collective-permute-start.1 = (bf16[256,768]{1,0:T(8,128)(2,1)S(1)}, bf16[256,768]{1,0:T(8,128)(2,1)}, u32[]{:S(2)}, u32[]{:S(2)}) collective-permute-start(bf16[256,768]{1,0:T(8,128)(2,1)S(1)} %get-tuple-element.179), channel_id=1, source_target_pairs={{0,3},{1,0},{2,1},{3,2},{4,7},{5,4},{6,5},{7,6},{8,11},{9,8},{10,9... | collective-permute-start | bytes 1179656 | tf_op jit(solution)/shard_map/ppermute | solution.py:29
  160.0 7.5 %collective-permute-start.2 = (bf16[256,768]{1,0:T(8,128)(2,1)}, bf16[256,768]{1,0:T(8,128)(2,1)}, u32[]{:S(2)}, u32[]{:S(2)}) collective-permute-start(bf16[256,768]{1,0:T(8,128)(2,1)} %collective-permute-done), channel_id=1, source_target_pairs={{0,1},{1,2},{2,3},{3,0},{4,5},{5,6},{6,7},{7,4},{8,9},{9,10},{10,1... | collective-permute-start | bytes 1179656 | tf_op jit(solution)/shard_map/ppermute | solution.py:24
Sparse Core Ops, SparseCore 0:
  10.2 46.8 all-gather.1
  110.6 36.2 reduce-scatter.2
  212.0 74.2 reduce-scatter.4
